TPU v7x, 32 devices: a whole 2x2x4 slice. The times are simulated.
32 devices in a mesh: groups: 2 (over y), seq: 4 (over z), mp: 4 (over x, core).
Axes of the slice: x: 2, y: 2, z: 4, core: 2. Of those that a mesh axis runs over, the one named last changes fastest.
Arguments:
- node_vectors: bfloat16 [1024, 2048], P(('groups', 'seq'), 'mp'), parts along dimension 0, may hold values from -6 to 6
- standardize_multiplier: float32 [2048], replicated, may hold values from 0.1 to 1.9
- probe_matrix: bfloat16 [2048, 1024], P(None, 'mp'), may hold values from -1 to 1
- lookup_matrix: bfloat16 [2048, 1024], P(None, 'mp'), may hold values from -1 to 1
- content_matrix: bfloat16 [2048, 1024], P(None, 'mp'), may hold values from -0.125 to 0.125
- softness_per_group: float32 [8], P('mp'), may hold values from 0.5 to 12
- exit_matrix: bfloat16 [1024, 2048], P('mp'), may hold values from -0.1875 to 0.1875
Outputs:
- mixed: bfloat16 [1024, 2048], P(('groups', 'seq'), 'mp'), parts along dimension 0
There are 2 independent parts, one for each index of `groups`. A program takes and returns all parts, laid end to end along the dimension named above; an argument that names none is the same for every part. Nothing has to cross between parts.
All inputs are finite; a program needn't handle non-finite values.
Results may differ from a plain program's by a relative error of at most 0.011.
Values may be sent and summed in bfloat16 or wider, within the bound.
A program may use at most 64 MiB of HBM per device.

v0:
```python
import math
import jax
import jax.numpy as jnp
from jax import lax
from jax.sharding import PartitionSpec as P


def attend(state_in, blocks, query_heads, inverse_root_span, resident_groups, channel_span):
    running_max, running_sum, weighted = state_in
    key_block, value_block = blocks
    count = key_block.shape[0]
    key_heads = key_block.reshape(count, resident_groups, channel_span)
    value_heads = value_block.reshape(count, resident_groups, channel_span)
    scores = (
        jnp.einsum("rhd,nhd->hrn", query_heads, key_heads, preferred_element_type=jnp.float32)
        * inverse_root_span[:, None, None]
    )
    new_max = jnp.max(scores, axis=-1)
    rescale = jnp.exp(running_max - new_max)
    weights = jnp.exp(scores - new_max[:, :, None])
    running_sum = running_sum * rescale + jnp.sum(weights, axis=-1)
    update = jnp.einsum(
        "hrn,nhd->hrd",
        weights.astype(jnp.bfloat16),
        value_heads,
        preferred_element_type=jnp.float32,
    )
    weighted = weighted * rescale[:, :, None] + update
    return (new_max, running_sum, weighted)


def per_device(
    node_vectors,
    standardize_multiplier,
    probe_matrix,
    lookup_matrix,
    content_matrix,
    softness_per_group,
    exit_matrix,
):
    full_rows = lax.all_gather(node_vectors, "mp", axis=1, tiled=True)
    widened = full_rows.astype(jnp.float32)
    average = jnp.mean(widened, axis=-1, keepdims=True)
    centered = widened - average
    variance = jnp.mean(centered * centered, axis=-1, keepdims=True)
    normed = (centered * lax.rsqrt(variance + 1e-05) * standardize_multiplier).astype(jnp.bfloat16)
    queries = jnp.dot(normed, probe_matrix, preferred_element_type=jnp.float32).astype(jnp.bfloat16)
    key_rows = jnp.dot(normed, lookup_matrix, preferred_element_type=jnp.float32).astype(
        jnp.bfloat16
    )
    value_rows = jnp.dot(normed, content_matrix, preferred_element_type=jnp.float32).astype(
        jnp.bfloat16
    )
    resident_groups = softness_per_group.shape[0]
    head_cols = queries.shape[1]
    channel_span = head_cols // resident_groups
    token_count = queries.shape[0]
    query_heads = queries.reshape(token_count, resident_groups, channel_span)
    inverse_root_span = softness_per_group / math.sqrt(channel_span)
    initial = (
        jnp.full((resident_groups, token_count), -jnp.inf, jnp.float32),
        jnp.zeros((resident_groups, token_count), jnp.float32),
        jnp.zeros((resident_groups, token_count, channel_span), jnp.float32),
    )
    final = attend(
        initial,
        (
            lax.all_gather(key_rows, "seq", axis=0, tiled=True),
            lax.all_gather(value_rows, "seq", axis=0, tiled=True),
        ),
        query_heads,
        inverse_root_span,
        resident_groups,
        channel_span,
    )
    heads_out = (
        (final[2] / final[1][:, :, None])
        .transpose(1, 0, 2)
        .reshape(token_count, head_cols)
        .astype(jnp.bfloat16)
    )
    partial_sums = jnp.dot(heads_out, exit_matrix, preferred_element_type=jnp.float32)
    summed = lax.psum_scatter(
        partial_sums.astype(jnp.bfloat16), "mp", scatter_dimension=1, tiled=True
    ).astype(jnp.float32)
    return (node_vectors.astype(jnp.float32) + summed).astype(jnp.bfloat16)


def solution(mesh):
    return jax.shard_map(
        per_device,
        mesh=mesh,
        in_specs=(
            P(("groups", "seq"), "mp"),
            P(),
            P(None, "mp"),
            P(None, "mp"),
            P(None, "mp"),
            P("mp"),
            P("mp", None),
        ),
        out_specs=P(("groups", "seq"), "mp"),
        check_vma=False,
    )
```

profile of v0, /device:TPU:0, one launch (start us, length us, event | category | flops | bytes accessed | tf_op | source)
XLA Modules:
  0.0 81.6 jit_solution(14585379958456140718)
XLA Ops:
  6.5 0.0 copy-start
  6.5 0.0 copy-start.2
  6.5 0.0 reduce-scatter.2.cloned.1.call-start
  6.5 0.8 broadcast_multiply_fusion
  7.3 8.8 %all_gather.9 = bf16[128,2048]{1,0:T(8,128)(2,1)S(1)} all-gather(bf16[128,512]{1,0:T(8,128)(2,1)} %param.7), channel_id=1, replica_groups=mesh['groups'=2,'seq'=4,'mp'=4] {'mp'}, dimensions={1}, use_global_device_ids=true | all-gather | bytes 655360 | tf_op jit(solution)/shard_map/all_gather | solution.py:41
  16.2 0.2 convert_reduce_fusion
  16.4 0.0 copy-start.5
  16.4 0.3 fusion.6
  16.7 0.0 copy-done.2
  16.7 0.4 copy-done.5
  17.1 0.0 copy-start.3
  17.1 0.4 convolution_convert_fusion.2
  17.4 0.9 %copy-done.3 = bf16[2048,256]{1,0:T(8,128)(2,1)S(1)} copy-done((bf16[2048,256]{1,0:T(8,128)(2,1)S(1)}, bf16[2048,256]{1,0:T(8,128)(2,1)}, u32[]{:S(2)}) %copy-start.3) | copy-done | bytes 1048600
  18.3 0.0 copy-start.4
  18.3 0.4 convolution_convert_fusion.1
  18.6 0.9 %copy-done.4 = bf16[2048,256]{1,0:T(8,128)(2,1)S(1)} copy-done((bf16[2048,256]{1,0:T(8,128)(2,1)S(1)}, bf16[2048,256]{1,0:T(8,128)(2,1)}, u32[]{:S(2)}) %copy-start.4) | copy-done | bytes 1048600
  19.5 0.4 fusion.5
  19.9 14.1 %all_gather.11 = bf16[512,256]{1,0:T(8,128)(2,1)S(1)} all-gather(bf16[128,256]{1,0:T(8,128)(2,1)S(1)} %convolution_convert_fusion.1), channel_id=1, replica_groups=mesh['groups'=2,'seq'=4,'mp'=4] {'seq'}, dimensions={0}, use_global_device_ids=true | all-gather | bytes 327680 | tf_op jit(solution)/shard_map/all_gather | solution.py:69
  34.0 0.1 copy.11
  34.1 14.6 %all_gather.10 = bf16[512,256]{1,0:T(8,128)(2,1)S(1)} all-gather(bf16[128,256]{1,0:T(8,128)(2,1)S(1)} %convolution_convert_fusion.2), channel_id=1, replica_groups=mesh['groups'=2,'seq'=4,'mp'=4] {'seq'}, dimensions={0}, use_global_device_ids=true | all-gather | bytes 327680 | tf_op jit(solution)/shard_map/all_gather | solution.py:68
  48.7 0.3 fusion.20
  49.1 0.2 fusion.9
  49.3 0.3 fusion.4
  49.6 0.0 copy-done
  49.6 1.1 %convolution_convert_fusion = bf16[128,2048]{1,0:T(8,128)(2,1)} fusion(bf16[128,256]{0,1:T(8,128)(2,1)S(1)} %bitcast.39, bf16[256,2048]{1,0:T(8,128)(2,1)S(1)} %copy-done), kind=kOutput, calls=%fused_computation | convolution fusion | flops 134479872 | bytes 1638400 | tf_op jit(solution)/shard_map/dot_general | solution.py:82
  50.8 0.0 copy-start.1
  50.8 0.0 reduce-scatter.2.cloned.1.call-update
  50.8 22.4 %reduce-scatter.2.cloned.1.call-done = bf16[128,512]{1,0:T(8,128)(2,1)} async-done(((bf16[128,2048]{1,0:T(8,128)(2,1)}), bf16[128,512]{1,0:T(8,128)(2,1)}) %reduce-scatter.2.cloned.1.call-update) | async-done | bytes 131088 | tf_op jit(solution)/shard_map/reduce_scatter | solution.py:83
  73.2 0.0 copy-done.1
  73.2 1.6 %add_convert_fusion = bf16[128,512]{1,0:T(8,128)(2,1)} fusion(bf16[128,512]{1,0:T(8,128)(2,1)} %reduce-scatter.2.cloned.1.call-done, bf16[128,512]{1,0:T(8,128)(2,1)S(1)} %copy-done.1), kind=kLoop, calls=%fused_computation.22 | loop fusion | flops 262144 | bytes 393216 | tf_op jit(solution)/shard_map/convert_element_type | solution.py:86
  (4 shorter events, 0.0 us)
Async XLA Ops:
  6.5 43.1 %copy-start = (bf16[256,2048]{1,0:T(8,128)(2,1)S(1)}, bf16[256,2048]{1,0:T(8,128)(2,1)}, u32[]{:S(2)}) copy-start(bf16[256,2048]{1,0:T(8,128)(2,1)} %param.13) | copy-start | bytes 3145732
  6.5 10.1 %copy-start.2 = (bf16[2048,256]{1,0:T(8,128)(2,1)S(1)}, bf16[2048,256]{1,0:T(8,128)(2,1)}, u32[]{:S(2)}) copy-start(bf16[2048,256]{1,0:T(8,128)(2,1)} %param.10) | copy-start | bytes 3145732
  6.5 66.6 %reduce-scatter.2.cloned.1.call-start = ((), (), s32[]{:S(2)}) async-start(), calls=%async_computation.1 | async-start | bytes 655360 | tf_op jit(solution)/shard_map/reduce_scatter | solution.py:83
  16.4 0.7 copy-start.5
  17.1 1.2 %copy-start.3 = (bf16[2048,256]{1,0:T(8,128)(2,1)S(1)}, bf16[2048,256]{1,0:T(8,128)(2,1)}, u32[]{:S(2)}) copy-start(bf16[2048,256]{1,0:T(8,128)(2,1)} %param.11) | copy-start | bytes 3145732
  18.3 1.2 %copy-start.4 = (bf16[2048,256]{1,0:T(8,128)(2,1)S(1)}, bf16[2048,256]{1,0:T(8,128)(2,1)}, u32[]{:S(2)}) copy-start(bf16[2048,256]{1,0:T(8,128)(2,1)} %param.9) | copy-start | bytes 3145732
  50.8 22.4 %copy-start.1 = (bf16[128,512]{1,0:T(8,128)(2,1)S(1)}, bf16[128,512]{1,0:T(8,128)(2,1)}, u32[]{:S(2)}) copy-start(bf16[128,512]{1,0:T(8,128)(2,1)} %param.7) | copy-start | bytes 393220
Sparse Core Ops, SparseCore 0:
  50.9 22.2 reduce-scatter.1
where the time goes:
time: 81.9 us; the launch traced here: 81.6 us
  blocking collectives  37.6 us (46%)
  waiting for transfers between devices  22.4 us (27%)
  between operations  13.5 us (16%)
  other arithmetic  3.1 us (4%)
  matrix products  2.85 us (3%)
  local copies, waits for them, and re-layouts  2.25 us (3%)
    reduce_scatter x1, waiting for transfers between devices, per_device(): lax.psum_scatter(partial_sums.astype(jnp.bfloat16), 'mp', scatter_dimensi...  22.4 us
    all_gather x1, blocking collectives, per_device(): lax.all_gather(key_rows, 'seq', axis=0, tiled=True)  14.6 us
    all_gather x1, blocking collectives, per_device(): lax.all_gather(value_rows, 'seq', axis=0, tiled=True)  14.1 us
    all_gather x1, blocking collectives, per_device(): full_rows = lax.all_gather(node_vectors, 'mp', axis=1, tiled=True)  8.84 us
    unnamed x12, local copies, waits for them, and re-layouts  2.11 us
  transfers between devices with their start and end apart: 1, of which 1 were waited for; matrix products, arithmetic and copies ran while one was open for 0% of the time, Pallas kernels for 0%

commit v1 on v0

--- a/solution.py
+++ b/solution.py
@@ -3,6 +3,23 @@
 import jax.numpy as jnp
 from jax import lax
 from jax.sharding import PartitionSpec as P
+
+
+def laid_out(pieces, dim):
+    pieces = jnp.moveaxis(pieces, 0, dim)
+    shape = pieces.shape
+    return pieces.reshape(*shape[:dim], shape[dim] * shape[dim + 1], *shape[dim + 2 :])
+
+
+def collect(x, axis, dim):
+    size = lax.axis_size(axis)
+    right = [(i, (i + 1) % size) for i in range(size)]
+    blocks = [x]
+    while len(blocks) < size:
+        blocks.append(lax.ppermute(blocks[-1], axis, right))
+    index = lax.axis_index(axis)
+    blocks = jnp.stack(blocks)[(index - jnp.arange(size)) % size]
+    return laid_out(blocks, dim)
 
 
 def attend(state_in, blocks, query_heads, inverse_root_span, resident_groups, channel_span):
@@ -64,10 +81,7 @@
     )
     final = attend(
         initial,
-        (
-            lax.all_gather(key_rows, "seq", axis=0, tiled=True),
-            lax.all_gather(value_rows, "seq", axis=0, tiled=True),
-        ),
+        (lax.all_gather(key_rows, "seq", axis=0, tiled=True), collect(value_rows, "seq", 0)),
         query_heads,
         inverse_root_span,
         resident_groups,

time: 81.9 us -> 77.3 us (0.944)
  blocking collectives: 37.6 us -> 23.1 us
  waiting for transfers between devices: 22.4 us -> 30.5 us
  starting transfers between devices: 0.01 us -> 2.93 us
    all_gather x1 -> x0, blocking collectives: 14.1 us -> none  [per_device(): lax.all_gather(value_rows, 'seq', axis=0, tiled=True)]
    ppermute x0 -> x3, waiting for transfers between devices: none -> 10.9 us  [collect(): blocks.append(lax.ppermute(blocks[-1], axis, right))]
    ppermute x0 -> x3, starting transfers between devices: none -> 2.93 us  [collect(): blocks.append(lax.ppermute(blocks[-1], axis, right))]
    reduce_scatter x1, waiting for transfers between devices: 22.4 us -> 19.6 us  [per_device(): lax.psum_scatter(partial_sums.astype(jnp.bfloat16), 'mp', scatter_dimensi...]
    unnamed x12 -> x14, local copies, waits for them, and re-layouts: 2.11 us -> 1.25 us
  transfers between devices with their start and end apart: 1 -> 4, of which waited for: 1 -> 3; matrix products, arithmetic and copies ran while one was open for 0% -> 2% of each run, Pallas kernels for 0% -> 0%
where the time goes in v1:
time: 77.3 us; the launch traced here: 77.1 us
  waiting for transfers between devices  30.5 us (39%)
  blocking collectives  23.1 us (30%)
  between operations  13.5 us (17%)
  starting transfers between devices  2.93 us (4%)
  matrix products  2.87 us (4%)
  other arithmetic  2.35 us (3%)
  local copies, waits for them, and re-layouts  1.88 us (2%)
    reduce_scatter x1, waiting for transfers between devices, per_device(): lax.psum_scatter(partial_sums.astype(jnp.bfloat16), 'mp', scatter_dimensi...  19.6 us
    all_gather x1, blocking collectives, per_device(): lax.all_gather(key_rows, 'seq', axis=0, tiled=True)  14.1 us
    ppermute x3, waiting for transfers between devices, collect(): blocks.append(lax.ppermute(blocks[-1], axis, right))  10.9 us
    all_gather x1, blocking collectives, per_device(): full_rows = lax.all_gather(node_vectors, 'mp', axis=1, tiled=True)  8.97 us
    ppermute x3, starting transfers between devices, collect(): blocks.append(lax.ppermute(blocks[-1], axis, right))  2.93 us
    convert_element_type x1, other arithmetic, per_device(): return (node_vectors.astype(jnp.float32) + summed).astype(jnp.bfloat16)  1.59 us
  transfers between devices with their start and end apart: 4, of which 3 were waited for; matrix products, arithmetic and copies ran while one was open for 2% of the time, Pallas kernels for 0%

profile of v1, /device:TPU:0, one launch (start us, length us, event | category | flops | bytes accessed | tf_op | source)
XLA Modules:
  0.0 77.1 jit_solution(11828307231579773752)
XLA Ops:
  6.5 0.0 copy-start
  6.5 0.0 copy-start.2
  6.5 0.0 reduce-scatter.2.cloned.1.call-start
  6.5 9.0 %all_gather.6 = bf16[128,2048]{1,0:T(8,128)(2,1)S(1)} all-gather(bf16[128,512]{1,0:T(8,128)(2,1)} %param.7), channel_id=1, replica_groups=mesh['groups'=2,'seq'=4,'mp'=4] {'mp'}, dimensions={1}, use_global_device_ids=true | all-gather | bytes 655360 | tf_op jit(solution)/shard_map/all_gather | solution.py:58
  15.5 0.2 convert_reduce_fusion
  15.7 0.0 copy-start.5
  15.7 0.3 fusion.6
  16.0 0.0 copy-done.2
  16.0 0.4 copy-done.5
  16.4 0.0 copy-start.6
  16.4 0.0 copy-start.3
  16.4 0.4 convolution_convert_fusion.1
  16.7 1.6 %collective-permute-start = (bf16[128,256]{1,0:T(8,128)(2,1)S(1)}, bf16[128,256]{1,0:T(8,128)(2,1)S(1)}, u32[]{:S(2)}, u32[]{:S(2)}) collective-permute-start(bf16[128,256]{1,0:T(8,128)(2,1)S(1)} %convolution_convert_fusion.1), channel_id=1, source_target_pairs={{0,4},{4,8},{8,12},{12,0},{1,5},{5,9},{9,13},{13,1},{2,6},{6,10},{... | collective-permute-start | bytes 196616 | tf_op jit(solution)/shard_map/ppermute | solution.py:19
  18.4 0.0 copy-done.6
  18.4 0.0 copy-done.3
  18.4 0.0 copy-start.4
  18.4 0.4 convolution_convert_fusion.2
  18.8 0.8 %copy-done.4 = bf16[2048,256]{1,0:T(8,128)(2,1)S(1)} copy-done((bf16[2048,256]{1,0:T(8,128)(2,1)S(1)}, bf16[2048,256]{1,0:T(8,128)(2,1)}, u32[]{:S(2)}) %copy-start.4) | copy-done | bytes 1048600
  19.6 0.4 fusion.5
  20.0 14.1 %all_gather.7 = bf16[512,256]{1,0:T(8,128)(2,1)S(1)} all-gather(bf16[128,256]{1,0:T(8,128)(2,1)S(1)} %convolution_convert_fusion.2), channel_id=1, replica_groups=mesh['groups'=2,'seq'=4,'mp'=4] {'seq'}, dimensions={0}, use_global_device_ids=true | all-gather | bytes 327680 | tf_op jit(solution)/shard_map/all_gather | solution.py:84
  34.1 0.3 fusion.23
  34.4 0.2 fusion.9
  34.7 0.0 collective-permute-done
  34.7 1.3 %collective-permute-start.1 = (bf16[128,256]{1,0:T(8,128)(2,1)S(1)}, bf16[128,256]{1,0:T(8,128)(2,1)S(1)}, u32[]{:S(2)}, u32[]{:S(2)}) collective-permute-start(bf16[128,256]{1,0:T(8,128)(2,1)S(1)} %collective-permute-done), channel_id=1, source_target_pairs={{0,4},{4,8},{8,12},{12,0},{1,5},{5,9},{9,13},{13,1},{2,6},{6,10},{... | collective-permute-start | bytes 196616 | tf_op jit(solution)/shard_map/ppermute | solution.py:19
  36.0 4.8 %collective-permute-done.1 = bf16[128,256]{1,0:T(8,128)(2,1)S(1)} collective-permute-done((bf16[128,256]{1,0:T(8,128)(2,1)S(1)}, bf16[128,256]{1,0:T(8,128)(2,1)S(1)}, u32[]{:S(2)}, u32[]{:S(2)}) %collective-permute-start.1) | collective-permute-done | bytes 65568 | tf_op jit(solution)/shard_map/ppermute | solution.py:19
  40.8 0.0 collective-permute-start.2
  40.8 6.1 %collective-permute-done.2 = bf16[128,256]{1,0:T(8,128)(2,1)S(1)} collective-permute-done((bf16[128,256]{1,0:T(8,128)(2,1)S(1)}, bf16[128,256]{1,0:T(8,128)(2,1)S(1)}, u32[]{:S(2)}, u32[]{:S(2)}) %collective-permute-start.2) | collective-permute-done | bytes 65568 | tf_op jit(solution)/shard_map/ppermute | solution.py:19
  46.9 0.6 gather_fusion
  47.5 0.1 reshape_reshape.3
  47.5 0.3 fusion.4
  47.9 0.0 copy-done
  47.9 1.1 %convolution_convert_fusion = bf16[128,2048]{1,0:T(8,128)(2,1)} fusion(bf16[128,256]{0,1:T(8,128)(2,1)S(1)} %bitcast.42, bf16[256,2048]{1,0:T(8,128)(2,1)S(1)} %copy-done), kind=kOutput, calls=%fused_computation.1 | convolution fusion | flops 134479872 | bytes 1638400 | tf_op jit(solution)/shard_map/dot_general | solution.py:96
  49.0 0.0 copy-start.1
  49.0 0.0 reduce-scatter.2.cloned.1.call-update
  49.0 19.6 %reduce-scatter.2.cloned.1.call-done = bf16[128,512]{1,0:T(8,128)(2,1)} async-done(((bf16[128,2048]{1,0:T(8,128)(2,1)}), bf16[128,512]{1,0:T(8,128)(2,1)}) %reduce-scatter.2.cloned.1.call-update) | async-done | bytes 131088 | tf_op jit(solution)/shard_map/reduce_scatter | solution.py:97
  68.6 0.0 copy-done.1
  68.6 1.6 %add_convert_fusion = bf16[128,512]{1,0:T(8,128)(2,1)} fusion(bf16[128,512]{1,0:T(8,128)(2,1)} %reduce-scatter.2.cloned.1.call-done, bf16[128,512]{1,0:T(8,128)(2,1)S(1)} %copy-done.1), kind=kLoop, calls=%fused_computation.25 | loop fusion | flops 262144 | bytes 393216 | tf_op jit(solution)/shard_map/convert_element_type | solution.py:100
  (8 shorter events, 0.1 us)
Async XLA Ops:
  6.5 41.3 %copy-start = (bf16[256,2048]{1,0:T(8,128)(2,1)S(1)}, bf16[256,2048]{1,0:T(8,128)(2,1)}, u32[]{:S(2)}) copy-start(bf16[256,2048]{1,0:T(8,128)(2,1)} %param.13) | copy-start | bytes 3145732
  6.5 9.4 %copy-start.2 = (bf16[2048,256]{1,0:T(8,128)(2,1)S(1)}, bf16[2048,256]{1,0:T(8,128)(2,1)}, u32[]{:S(2)}) copy-start(bf16[2048,256]{1,0:T(8,128)(2,1)} %param.11) | copy-start | bytes 3145732
  6.5 62.1 %reduce-scatter.2.cloned.1.call-start = ((), (), s32[]{:S(2)}) async-start(), calls=%async_computation.1 | async-start | bytes 655360 | tf_op jit(solution)/shard_map/reduce_scatter | solution.py:97
  15.7 0.7 copy-start.5
  16.4 2.0 %copy-start.6 = (f32[2]{0:T(128)S(1)}, f32[2]{0:T(128)}, u32[]{:S(2)}) copy-start(f32[2]{0:T(128)} %param.12) | copy-start | bytes 28
  16.4 2.0 %copy-start.3 = (bf16[2048,256]{1,0:T(8,128)(2,1)S(1)}, bf16[2048,256]{1,0:T(8,128)(2,1)}, u32[]{:S(2)}) copy-start(bf16[2048,256]{1,0:T(8,128)(2,1)} %param.10) | copy-start | bytes 3145732
  16.7 17.9 %collective-permute-start = (bf16[128,256]{1,0:T(8,128)(2,1)S(1)}, bf16[128,256]{1,0:T(8,128)(2,1)S(1)}, u32[]{:S(2)}, u32[]{:S(2)}) collective-permute-start(bf16[128,256]{1,0:T(8,128)(2,1)S(1)} %convolution_convert_fusion.1), channel_id=1, source_target_pairs={{0,4},{4,8},{8,12},{12,0},{1,5},{5,9},{9,13},{13,1},{2,6},{6,10},{... | collective-permute-start | bytes 196616 | tf_op jit(solution)/shard_map/ppermute | solution.py:19
  18.4 1.2 %copy-start.4 = (bf16[2048,256]{1,0:T(8,128)(2,1)S(1)}, bf16[2048,256]{1,0:T(8,128)(2,1)}, u32[]{:S(2)}) copy-start(bf16[2048,256]{1,0:T(8,128)(2,1)} %param.9) | copy-start | bytes 3145732
  34.7 6.1 %collective-permute-start.1 = (bf16[128,256]{1,0:T(8,128)(2,1)S(1)}, bf16[128,256]{1,0:T(8,128)(2,1)S(1)}, u32[]{:S(2)}, u32[]{:S(2)}) collective-permute-start(bf16[128,256]{1,0:T(8,128)(2,1)S(1)} %collective-permute-done), channel_id=1, source_target_pairs={{0,4},{4,8},{8,12},{12,0},{1,5},{5,9},{9,13},{13,1},{2,6},{6,10},{... | collective-permute-start | bytes 196616 | tf_op jit(solution)/shard_map/ppermute | solution.py:19
  40.8 6.1 %collective-permute-start.2 = (bf16[128,256]{1,0:T(8,128)(2,1)S(1)}, bf16[128,256]{1,0:T(8,128)(2,1)S(1)}, u32[]{:S(2)}, u32[]{:S(2)}) collective-permute-start(bf16[128,256]{1,0:T(8,128)(2,1)S(1)} %collective-permute-done.1), channel_id=1, source_target_pairs={{0,4},{4,8},{8,12},{12,0},{1,5},{5,9},{9,13},{13,1},{2,6},{6,10},{... | collective-permute-start | bytes 196616 | tf_op jit(solution)/shard_map/ppermute | solution.py:19
  49.0 19.7 %copy-start.1 = (bf16[128,512]{1,0:T(8,128)(2,1)S(1)}, bf16[128,512]{1,0:T(8,128)(2,1)}, u32[]{:S(2)}) copy-start(bf16[128,512]{1,0:T(8,128)(2,1)} %param.7) | copy-start | bytes 393220
Sparse Core Ops, SparseCore 0:
  49.1 19.4 reduce-scatter.1
